TPU v7x, 32 devices: a whole 2x2x4 slice. The times are simulated.
32 devices in a mesh: sec: 2 (over core), blk: 8 (over z, x), ch: 2 (over y).
Axes of the slice: x: 2, y: 2, z: 4, core: 2. Of those that a mesh axis runs over, the one named last changes fastest.
Arguments:
- voltages: bfloat16 [123, 4096, 2048], P(None, 'blk', ('sec', 'ch')), may hold values from -6 to 6
Outputs:
- visibilities: bfloat16 [16, 2, 4096, 4096], P(('sec', 'ch'), None, 'blk')
All inputs are finite; a program needn't handle non-finite values.
Results may differ from a plain program's by a relative error of at most 0.0082.
Values may be sent and summed in bfloat16 or wider, within the bound.
A program may use at most 384 MiB of HBM per device.

v0:
```python
import math

import jax
import jax.numpy as jnp
from jax import lax
from jax.sharding import PartitionSpec as P

FFT = 2048
TAPS = 4
CH_GRP = 4


def make_window(tap_count, frame_len):
    position = jnp.arange(tap_count * frame_len, dtype=jnp.float32)
    offset = (position - tap_count * frame_len / 2 + 0.5) / frame_len
    taper = 0.5 - 0.5 * jnp.cos(2.0 * jnp.pi * (position + 0.5) / (tap_count * frame_len))
    profile = jnp.sinc(offset) * taper
    profile = profile * jnp.sqrt(frame_len / jnp.sum(profile * profile))
    return profile.reshape(tap_count, frame_len)


def dft_table(frame_len, chan_count, bank_size):
    spacing = bank_size // chan_count
    chosen = jnp.arange(chan_count, dtype=jnp.int32) * spacing + spacing // 2
    phases = jnp.arange(frame_len, dtype=jnp.int32)[:, None] * chosen[None, :] % frame_len
    angles = 2.0 * jnp.pi / frame_len * phases.astype(jnp.float32)
    factor = 1.0 / math.sqrt(frame_len)
    weights = jnp.stack([jnp.cos(angles) * factor, -jnp.sin(angles) * factor], axis=-1)
    return weights.reshape(frame_len, chan_count * 2).astype(jnp.bfloat16)


def pair_block(local_panel, remote_panel, steps):
    grams = jnp.einsum(
        "crti,cqtj->crqij", local_panel, remote_panel, preferred_element_type=jnp.float32
    )
    real_sum = grams[:, 0, 0] + grams[:, 1, 1]
    imag_sum = grams[:, 1, 0] - grams[:, 0, 1]
    return jnp.stack([real_sum, imag_sum], axis=1) / steps


def body(voltages):
    groups = lax.axis_size("sec") * lax.axis_size("ch")
    span_len = voltages.shape[2]
    panel_len = voltages.shape[1]
    steps = voltages.shape[0] - TAPS + 1
    chan_total = CH_GRP * groups
    group_pos = lax.axis_index("sec") * lax.axis_size("ch") + lax.axis_index("ch")
    first = group_pos * span_len
    window = lax.dynamic_slice_in_dim(make_window(TAPS, FFT), first, span_len, 1)
    summed = jnp.zeros((steps, panel_len, span_len), jnp.float32)
    for tap_index in range(TAPS):
        summed = summed + window[tap_index] * voltages[tap_index : tap_index + steps].astype(
            jnp.float32
        )
    filtered = summed.astype(jnp.bfloat16)
    weights = lax.dynamic_slice_in_dim(dft_table(FFT, chan_total, FFT // 2), first, span_len, 0)
    terms = jnp.einsum("tsn,nk->kts", filtered, weights, preferred_element_type=jnp.float32)
    spectra = lax.psum_scatter(
        terms.reshape(CH_GRP * lax.axis_size(("sec", "ch")), 2, steps, panel_len),
        ("sec", "ch"),
        scatter_dimension=0,
        tiled=True,
    ).astype(jnp.bfloat16)
    block = pair_block(spectra, lax.all_gather(spectra, "blk", axis=3, tiled=True), steps)
    return block.astype(jnp.bfloat16)


def solution(mesh):
    return jax.shard_map(
        body,
        mesh=mesh,
        in_specs=(P(None, "blk", ("sec", "ch")),),
        out_specs=P(("sec", "ch"), None, "blk", None),
        check_vma=False,
    )
```

profile of v0, /device:TPU:0, one launch (start us, length us, event | category | flops | bytes accessed | tf_op | source)
XLA Modules:
  0.0 491.0 jit_solution(1568423521587529917)
XLA Ops:
  6.5 0.0 reduce-scatter.2.cloned.1.call-start
  6.5 0.8 fusion.49
  7.4 0.1 select_select_fusion
  7.5 0.1 multiply_add_fusion.1
  8.3 0.1 fusion.52
  8.4 0.6 multiply_convert_fusion.1
  9.0 0.1 copy.10
  9.2 0.1 convert_element_type.47
  9.2 82.8 %fusion.1 = f32[32,120,512]{2,0,1:T(8,128)} fusion(bf16[123,512,512]{2,1,0:T(8,128)(2,1)} %param.1, f32[512]{0:T(512)S(1)} %bitcast.42, f32[512]{0:T(512)S(1)} %bitcast.40, f32[512]{0:T(512)S(1)} %bitcast.41, f32[512]{0:T(512)S(1)} %bitcast.39, bf16[2048,32]{0,1:T(8,128)(2,1)S(1)} %convert_element_type.47, s32[]{:T(128)S(6)} %select_n.62), kind=kOutput, calls=%fused_computation.3 | convolution fusion | flops 2390753280 | bytes 259563520 | tf_op jit(solution)/shard_map/tsn,nk->kts/dot_general | solution.py:57
  92.0 10.9 %copy.17 = f32[32,120,512]{2,1,0:T(8,128)} copy(f32[32,120,512]{2,0,1:T(8,128)} %fusion.1) | data formatting | bytes 15728640 | tf_op jit(solution)/shard_map/reshape | solution.py:59
  102.9 0.0 reduce-scatter.2.cloned.1.call-update
  102.9 0.2 all-gather.2.cloned.1.call-start
  103.1 71.6 %reduce-scatter.2.cloned.1.call-done = f32[4,2,120,512]{3,2,1,0:T(8,128)} async-done(((f32[16,2,120,512]{3,2,1,0:T(8,128)}), f32[4,2,120,512]{3,2,1,0:T(8,128)}) %reduce-scatter.2.cloned.1.call-update) | async-done | bytes 1966096 | tf_op jit(solution)/shard_map/reduce_scatter | solution.py:58
  174.7 2.6 convert_element_type.53
  177.4 0.0 all-gather.2.cloned.1.call-update
  177.4 119.1 %all-gather.2.cloned.1.call-done = bf16[4,2,120,4096]{3,2,1,0:T(8,128)(2,1)} async-done(((bf16[4,2,120,512]{3,2,1,0:T(8,128)(2,1)}), bf16[4,2,120,4096]{3,2,1,0:T(8,128)(2,1)}) %all-gather.2.cloned.1.call-update) | async-done | bytes 7864336 | tf_op jit(solution)/shard_map/all_gather | solution.py:64
  296.5 47.8 %convolution_bitcast_fusion = f32[4,2,2,512,4096]{3,4,1,2,0:T(8,128)} fusion(bf16[4,2,120,4096]{3,2,1,0:T(8,128)(2,1)} %all-gather.2.cloned.1.call-done, bf16[4,2,120,512]{3,2,1,0:T(8,128)(2,1)} %convert_element_type.53), kind=kOutput, calls=%fused_computation.4 | convolution fusion | flops 8053063680 | bytes 143065088 | tf_op jit(solution)/shard_map/crti,cqtj->crqij/dot_general | solution.py:33
  344.3 33.2 %fusion.2 = f32[4,1,512,4096]{2,3,0,1:T(8,128)} fusion(f32[4,2,2,512,4096]{3,4,1,2,0:T(8,128)} %convolution_bitcast_fusion), kind=kLoop, calls=%fused_computation.6 | loop fusion | flops 8388608 | bytes 100663296 | tf_op jit(solution)/shard_map/sub | solution.py:37
  377.5 33.1 %fusion.4 = f32[4,1,512,4096]{2,3,0,1:T(8,128)} fusion(f32[4,2,2,512,4096]{3,4,1,2,0:T(8,128)} %convolution_bitcast_fusion), kind=kLoop, calls=%fused_computation.9 | loop fusion | flops 8388608 | bytes 100663296 | tf_op jit(solution)/shard_map/add | solution.py:36
  410.6 32.9 %fusion = bf16[4,2,512,4096]{2,3,0,1:T(8,128)(2,1)} fusion(f32[4,1,512,4096]{2,3,0,1:T(8,128)} %fusion.2, f32[4,1,512,4096]{2,3,0,1:T(8,128)} %fusion.4), kind=kLoop, calls=%fused_computation.2 | loop fusion | flops 50331648 | bytes 100663296 | tf_op jit(solution)/shard_map/convert_element_type | solution.py:65
  443.5 40.6 %copy.14 = bf16[4,2,512,4096]{3,2,1,0:T(8,128)(2,1)} copy(bf16[4,2,512,4096]{2,3,0,1:T(8,128)(2,1)} %fusion) | data formatting | bytes 67108864 | tf_op jit(solution)/shard_map/convert_element_type | solution.py:65
  (5 shorter events, 0.1 us)
Async XLA Ops:
  6.5 168.2 %reduce-scatter.2.cloned.1.call-start = ((), (), s32[]{:S(2)}) async-start(), calls=%async_computation.1 | async-start | bytes 9830400 | tf_op jit(solution)/shard_map/reduce_scatter | solution.py:58
  102.9 193.6 %all-gather.2.cloned.1.call-start = ((), (), s32[]{:S(2)}) async-start(), calls=%async_computation.2 | async-start | bytes 8847360 | tf_op jit(solution)/shard_map/all_gather | solution.py:64
Sparse Core Ops, SparseCore 0:
  103.0 71.6 reduce-scatter.1
  177.5 118.9 all-gather.1
where the time goes:
time: 492 us; the launch traced here: 491 us
  waiting for transfers between devices  191 us (39%)
  matrix products  131 us (27%)
  other arithmetic  104 us (21%)
  local copies, waits for them, and re-layouts  51.7 us (11%)
  between operations  14.2 us (3%)
    all_gather x1, waiting for transfers between devices, body(): lax.all_gather(spectra, 'blk', axis=3, tiled=True)  119 us
    dot_general x1, matrix products, body(): jnp.einsum('tsn,nk->kts', filtered, weights, preferred_element_type=jnp.f...  82.8 us
    reduce_scatter x1, waiting for transfers between devices, body(): lax.psum_scatter(terms.reshape(CH_GRP * lax.axis_size(('sec', 'ch')), 2,...  71.6 us
    dot_general x1, matrix products, pair_block(): jnp.einsum('crti,cqtj->crqij', local_panel, remote_panel, preferred_eleme...  47.8 us
    convert_element_type x1, local copies, waits for them, and re-layouts, body(): return block.astype(jnp.bfloat16)  40.6 us
    sub x1, other arithmetic, pair_block(): imag_sum = grams[:, 1, 0] - grams[:, 0, 1]  33.2 us
    add x1, other arithmetic, pair_block(): real_sum = grams[:, 0, 0] + grams[:, 1, 1]  33.1 us
    convert_element_type x1, other arithmetic, body(): return block.astype(jnp.bfloat16)  32.9 us
  transfers between devices with their start and end apart: 2, of which 2 were waited for; matrix products, arithmetic and copies ran while one was open for 0% of the time, Pallas kernels for 0%

commit v1 on v0

v1 whole, which is shorter than its diff:
```python
import functools
import math

import jax
import jax.numpy as jnp
from jax import lax
from jax.experimental import pallas as pl
from jax.experimental.pallas import tpu as pltpu
from jax.sharding import PartitionSpec as P

FFT = 2048
TAPS = 4
CH_GRP = 4
LANES = 128


def make_window(tap_count, frame_len):
    position = jnp.arange(tap_count * frame_len, dtype=jnp.float32)
    offset = (position - tap_count * frame_len / 2 + 0.5) / frame_len
    taper = 0.5 - 0.5 * jnp.cos(2.0 * jnp.pi * (position + 0.5) / (tap_count * frame_len))
    profile = jnp.sinc(offset) * taper
    profile = profile * jnp.sqrt(frame_len / jnp.sum(profile * profile))
    return profile.reshape(tap_count, frame_len)


def dft_rows(first, span_len, frame_len, chan_count, bank_size):
    spacing = bank_size // chan_count
    row = jnp.arange(2 * chan_count, dtype=jnp.int32)
    chosen = row // 2 * spacing + spacing // 2
    sample = first + jnp.arange(span_len, dtype=jnp.int32)
    phases = chosen[:, None] * sample[None, :] % frame_len
    angles = 2.0 * jnp.pi / frame_len * phases.astype(jnp.float32)
    factor = 1.0 / math.sqrt(frame_len)
    wave = jnp.where(row[:, None] % 2 == 0, jnp.cos(angles), -jnp.sin(angles)) * factor
    return wave.astype(jnp.bfloat16).astype(jnp.float32)


def bank_kernel(steps, chunk, volts_ref, weights_ref, out_ref, products):
    part = pl.program_id(1)
    rows = weights_ref.shape[0] // TAPS
    weights = weights_ref[...]

    for frame in range(chunk):
        products[part * chunk + frame] = lax.dot_general(
            weights,
            volts_ref[frame],
            (((1,), (1,)), ((), ())),
            preferred_element_type=jnp.float32,
        )

    def add_taps(step, carry):
        total = products[step, 0:rows]
        for tap in range(1, TAPS):
            total = total + products[step + tap, tap * rows : (tap + 1) * rows]
        out_ref[pl.ds(step, rows, stride=steps), :] = total
        return carry

    low = jnp.maximum(part * chunk - (TAPS - 1), 0)
    lax.fori_loop(low, (part + 1) * chunk - (TAPS - 1), add_taps, 0)


def filter_bank(voltages, weights):
    frames, panel_len, span_len = voltages.shape
    steps = frames - TAPS + 1
    rows = weights.shape[0] // TAPS
    chunk = next(size for size in (41, 3, 1) if frames % size == 0)
    return pl.pallas_call(
        functools.partial(bank_kernel, steps, chunk),
        grid=(panel_len // LANES, frames // chunk),
        in_specs=[
            pl.BlockSpec((chunk, LANES, span_len), lambda s, f: (f, s, 0)),
            pl.BlockSpec(weights.shape, lambda s, f: (0, 0)),
        ],
        out_specs=pl.BlockSpec((rows * steps, LANES), lambda s, f: (0, s)),
        out_shape=jax.ShapeDtypeStruct((rows * steps, panel_len), jnp.float32),
        scratch_shapes=[pltpu.VMEM((frames, weights.shape[0], LANES), jnp.float32)],
        compiler_params=pltpu.CompilerParams(vmem_limit_bytes=48 * 1024 * 1024),
    )(voltages, weights)


def pair_kernel(steps, local_ref, remote_ref, out_ref, lhs):
    panel_len = local_ref.shape[2]

    @pl.when(pl.program_id(1) == 0)
    def _():
        turned = local_ref[0].astype(jnp.float32).T
        lhs[0:panel_len, :] = turned.astype(jnp.bfloat16)
        other = jnp.concatenate([turned[:, steps:], -turned[:, :steps]], axis=1)
        lhs[panel_len:, :] = other.astype(jnp.bfloat16)

    sums = jnp.dot(lhs[...], remote_ref[0, 0], preferred_element_type=jnp.float32)
    scaled = (sums * (1.0 / steps)).astype(jnp.bfloat16)
    out_ref[0, 0] = scaled[:panel_len]
    out_ref[0, 1] = scaled[panel_len:]


def correlate(local, gathered):
    chans, depth, panel_len = local.shape
    panels = gathered.shape[0]
    return pl.pallas_call(
        functools.partial(pair_kernel, depth // 2),
        grid=(chans, panels),
        in_specs=[
            pl.BlockSpec((1, depth, panel_len), lambda c, j: (c, 0, 0)),
            pl.BlockSpec((1, 1, depth, panel_len), lambda c, j: (j, c, 0, 0)),
        ],
        out_specs=pl.BlockSpec((1, 2, panel_len, panel_len), lambda c, j: (c, 0, 0, j)),
        out_shape=jax.ShapeDtypeStruct((chans, 2, panel_len, panels * panel_len), jnp.bfloat16),
        scratch_shapes=[pltpu.VMEM((2 * panel_len, depth), jnp.bfloat16)],
        compiler_params=pltpu.CompilerParams(vmem_limit_bytes=32 * 1024 * 1024),
    )(local, gathered)


def body(voltages):
    groups = lax.axis_size("sec") * lax.axis_size("ch")
    frames, panel_len, span_len = voltages.shape
    steps = frames - TAPS + 1
    chan_total = CH_GRP * groups
    group_pos = lax.axis_index("sec") * lax.axis_size("ch") + lax.axis_index("ch")
    first = group_pos * span_len
    window = lax.dynamic_slice_in_dim(make_window(TAPS, FFT), first, span_len, 1)
    table = dft_rows(first, span_len, FFT, chan_total, FFT // 2)
    weights = (window[:, None, :] * table[None]).astype(jnp.bfloat16)
    terms = filter_bank(voltages, weights.reshape(TAPS * 2 * chan_total, span_len))
    spectra = lax.psum_scatter(
        terms.reshape(chan_total, 2 * steps, panel_len),
        ("sec", "ch"),
        scatter_dimension=0,
        tiled=True,
    ).astype(jnp.bfloat16)
    return correlate(spectra, lax.all_gather(spectra, "blk", axis=0))


def solution(mesh):
    return jax.shard_map(
        body,
        mesh=mesh,
        in_specs=(P(None, "blk", ("sec", "ch")),),
        out_specs=P(("sec", "ch"), None, "blk", None),
        check_vma=False,
    )
```

time: 492 us -> 269 us (0.55)
  matrix products: 131 us -> 0 us
  other arithmetic: 104 us -> 4.1 us
  Pallas kernels: 0 us -> 55.6 us
  local copies, waits for them, and re-layouts: 51.7 us -> 4.43 us
    dot_general x2 -> x0, matrix products: 131 us -> none  [the longest x1 82.8 us: body(): jnp.einsum('tsn,nk->kts', filtered, weights, preferred_element_type=jnp.f...]
    pallas_call x0 -> x2, Pallas kernels: none -> 55.6 us  [the longest x1 31.6 us: filter_bank(): pl.pallas_call(functools.partial(bank_kernel, steps, chunk), grid=(panel_...]
    convert_element_type x2 -> x0, local copies, waits for them, and re-layouts: 40.7 us -> none  [the longest x1 40.6 us: body(): return block.astype(jnp.bfloat16)]
    sub x1 -> x0, other arithmetic: 33.2 us -> none  [pair_block(): imag_sum = grams[:, 1, 0] - grams[:, 0, 1]]
    add x2, other arithmetic: 33.1 us -> 0.01 us  [the longest x1 0.01 us: dft_rows(): chosen = row // 2 * spacing + spacing // 2]
    convert_element_type x2 -> x3, other arithmetic: 35.5 us -> 2.99 us  [the longest x1 2.63 us: body(): spectra = lax.psum_scatter(terms.reshape(chan_total, 2 * steps, panel_len...]
    reshape x1 -> x0, local copies, waits for them, and re-layouts: 10.9 us -> none  [body(): terms.reshape(CH_GRP * lax.axis_size(('sec', 'ch')), 2, steps, panel_len)]
where the time goes in v1:
time: 269 us
  waiting for transfers between devices  190 us (71%)
  Pallas kernels  55.6 us (21%)
  between operations  14.2 us (5%)
  local copies, waits for them, and re-layouts  4.43 us (2%)
  other arithmetic  4.1 us (2%)
    all_gather x1, waiting for transfers between devices, body(): return correlate(spectra, lax.all_gather(spectra, 'blk', axis=0))  119 us
    reduce_scatter x1, waiting for transfers between devices, body(): lax.psum_scatter(terms.reshape(chan_total, 2 * steps, panel_len), ('sec',...  71.8 us
    pallas_call x1, Pallas kernels, filter_bank(): pl.pallas_call(functools.partial(bank_kernel, steps, chunk), grid=(panel_...  31.6 us
    pallas_call x1, Pallas kernels, correlate(): pl.pallas_call(functools.partial(pair_kernel, depth // 2), grid=(chans, p...  24 us
  transfers between devices with their start and end apart: 2, of which 2 were waited for; matrix products, arithmetic and copies ran while one was open for 0% of the time, Pallas kernels for 0%

profile of v1, /device:TPU:0, one launch (start us, length us, event | category | flops | bytes accessed | tf_op | source)
XLA Modules:
  0.0 268.8 jit_solution(550007796486418591)
XLA Ops:
  6.5 0.0 reduce-scatter.2.cloned.1.call-start
  6.5 0.8 fusion.38
  7.4 0.1 select_select_fusion
  7.5 0.1 multiply_add_fusion.1
  8.3 0.3 fusion.5
  8.7 0.1 fusion.41
  8.8 31.6 %shard_map.17 = f32[3840,512]{1,0:T(8,128)} custom-call(bf16[123,512,512]{2,1,0:T(8,128)(2,1)} %volts_ref.1, bf16[128,512]{1,0:T(8,128)(2,1)S(1)} %bitcast.4), custom_call_target="tpu_custom_call" | custom-call | tf_op jit(solution)/shard_map/pallas_call | solution.py:67
  40.4 0.0 reduce-scatter.2.cloned.1.call-update
  40.4 0.0 all-gather.3.cloned.1.call-start
  40.5 71.8 %reduce-scatter.2.cloned.1.call-done = f32[4,240,512]{2,1,0:T(8,128)} async-done(((f32[16,240,512]{2,1,0:T(8,128)}), f32[4,240,512]{2,1,0:T(8,128)}) %reduce-scatter.2.cloned.1.call-update) | async-done | bytes 1966096 | tf_op jit(solution)/shard_map/reduce_scatter | solution.py:125
  112.3 2.6 convert_element_type.41.local_ref
  114.9 0.0 all-gather.3.cloned.1.call-update
  114.9 118.5 %all-gather.3.cloned.1.call-done = bf16[32,240,512]{2,1,0:T(8,128)(2,1)} async-done(((bf16[4,240,512]{2,1,0:T(8,128)(2,1)}), bf16[32,240,512]{2,1,0:T(8,128)(2,1)}) %all-gather.3.cloned.1.call-update) | async-done | bytes 7864336 | tf_op jit(solution)/shard_map/all_gather | solution.py:131
  233.5 0.0 copy-start
  233.5 1.2 copy-done
  234.7 0.0 copy-start.1
  234.7 3.2 %copy-done.1 = bf16[32,240,512]{2,1,0:T(8,128)(2,1)S(1)} copy-done((bf16[32,240,512]{2,1,0:T(8,128)(2,1)S(1)}, bf16[32,240,512]{2,1,0:T(8,128)(2,1)}, u32[]{:S(2)}) %copy-start.1) | copy-done | bytes 7864344
  237.9 24.0 %shard_map.18 = bf16[4,2,512,4096]{3,2,1,0:T(8,128)(2,1)} custom-call(bf16[4,240,512]{2,1,0:T(8,128)(2,1)S(1)} %copy-done, bf16[8,4,240,512]{3,2,1,0:T(8,128)(2,1)S(1)} %bitcast.3), custom_call_target="tpu_custom_call" | custom-call | tf_op jit(solution)/shard_map/pallas_call | solution.py:100
  (6 shorter events, 0.1 us)
Async XLA Ops:
  6.5 105.7 %reduce-scatter.2.cloned.1.call-start = ((), (), s32[]{:S(2)}) async-start(), calls=%async_computation.1 | async-start | bytes 9830400 | tf_op jit(solution)/shard_map/reduce_scatter | solution.py:125
  40.4 193.0 %all-gather.3.cloned.1.call-start = ((), (), s32[]{:S(2)}) async-start(), calls=%async_computation.2 | async-start | bytes 8847360 | tf_op jit(solution)/shard_map/all_gather | solution.py:131
  233.5 1.2 copy-start
  234.7 3.2 %copy-start.1 = (bf16[32,240,512]{2,1,0:T(8,128)(2,1)S(1)}, bf16[32,240,512]{2,1,0:T(8,128)(2,1)}, u32[]{:S(2)}) copy-start(bf16[32,240,512]{2,1,0:T(8,128)(2,1)} %all-gather.3.cloned.1.call-done) | copy-start | bytes 23592964
Sparse Core Ops, SparseCore 0:
  40.5 71.6 reduce-scatter.1
  115.0 118.3 all-gather.2

commit v2 on v1

--- a/solution.py
+++ b/solution.py
@@ -12,6 +12,7 @@
 TAPS = 4
 CH_GRP = 4
 LANES = 128
+MESH = pl.DeviceIdType.MESH
 
 
 def make_window(tap_count, frame_len):
@@ -35,7 +36,7 @@
     return wave.astype(jnp.bfloat16).astype(jnp.float32)
 
 
-def bank_kernel(steps, chunk, volts_ref, weights_ref, out_ref, products):
+def bank_kernel(steps, chunk, volts_ref, weights_ref, out_ref, products, spectra):
     part = pl.program_id(1)
     rows = weights_ref.shape[0] // TAPS
     weights = weights_ref[...]
@@ -52,11 +53,15 @@
         total = products[step, 0:rows]
         for tap in range(1, TAPS):
             total = total + products[step + tap, tap * rows : (tap + 1) * rows]
-        out_ref[pl.ds(step, rows, stride=steps), :] = total
+        spectra[pl.ds(step, rows, stride=steps), :] = total
         return carry
 
     low = jnp.maximum(part * chunk - (TAPS - 1), 0)
     lax.fori_loop(low, (part + 1) * chunk - (TAPS - 1), add_taps, 0)
+
+    @pl.when(part == pl.num_programs(1) - 1)
+    def _():
+        out_ref[0] = spectra[...].astype(jnp.bfloat16)
 
 
 def filter_bank(voltages, weights):
@@ -71,38 +76,178 @@
             pl.BlockSpec((chunk, LANES, span_len), lambda s, f: (f, s, 0)),
             pl.BlockSpec(weights.shape, lambda s, f: (0, 0)),
         ],
-        out_specs=pl.BlockSpec((rows * steps, LANES), lambda s, f: (0, s)),
-        out_shape=jax.ShapeDtypeStruct((rows * steps, panel_len), jnp.float32),
-        scratch_shapes=[pltpu.VMEM((frames, weights.shape[0], LANES), jnp.float32)],
+        out_specs=pl.BlockSpec((1, rows * steps, LANES), lambda s, f: (s, 0, 0)),
+        out_shape=jax.ShapeDtypeStruct((panel_len // LANES, rows * steps, LANES), jnp.bfloat16),
+        scratch_shapes=[
+            pltpu.VMEM((frames, weights.shape[0], LANES), jnp.float32),
+            pltpu.VMEM((rows * steps, LANES), jnp.float32),
+        ],
         compiler_params=pltpu.CompilerParams(vmem_limit_bytes=48 * 1024 * 1024),
     )(voltages, weights)
 
 
+def spread_kernel(n, terms_ref, all_ref, own_ref, got_core, half, got_chip, core_sems, chip_sems,
+                  ring_send, ring_recv, local_sems):
+    sec, ch, blk = lax.axis_index("sec"), lax.axis_index("ch"), lax.axis_index("blk")
+    other_sec, other_ch = 1 - sec, 1 - ch
+    chunks = terms_ref.shape[0]
+    group = own_ref.shape[1]
+    hops = n // 2
+
+    def block_at(place):
+        place = lax.rem(place + 2 * n, n)
+        return 2 * place + place // (n // 2) * (2 * n - 1 - 4 * place)
+
+    place = blk // 2 + lax.rem(blk, 2) * (n - 1 - 2 * (blk // 2))
+    sides = (block_at(place + 1), block_at(place - 1))
+
+    barrier = pltpu.get_barrier_semaphore()
+    partners = ({"sec": other_sec}, {"ch": other_ch}, {"blk": sides[0]}, {"blk": sides[1]})
+    for partner in partners:
+        pl.semaphore_signal(barrier, inc=1, device_id=partner, device_id_type=MESH)
+    pl.semaphore_wait(barrier, len(partners))
+
+    def core_copy(q):
+        return pltpu.make_async_remote_copy(
+            src_ref=terms_ref.at[q, pl.ds(other_sec * 2 * group, 2 * group)],
+            dst_ref=got_core.at[q],
+            send_sem=core_sems.at[0, q],
+            recv_sem=core_sems.at[1, q],
+            device_id={"sec": other_sec},
+            device_id_type=MESH,
+        )
+
+    def chip_copy(q):
+        return pltpu.make_async_remote_copy(
+            src_ref=half.at[q],
+            dst_ref=got_chip.at[q],
+            send_sem=chip_sems.at[0, q],
+            recv_sem=chip_sems.at[1, q],
+            device_id={"ch": other_ch},
+            device_id_type=MESH,
+        )
+
+    def ring_copy(q, side, hop):
+        origin = block_at(place - (hop - 1) * (1 - 2 * side))
+        source = own_ref.at[q] if hop == 1 else all_ref.at[origin, q]
+        target = all_ref.at[origin, q]
+        if hop == hops:
+            piece = pl.ds(side * (group // 2), group // 2)
+            source, target = source.at[piece], target.at[piece]
+        return pltpu.make_async_remote_copy(
+            src_ref=source,
+            dst_ref=target,
+            send_sem=ring_send.at[side, hop - 1, q],
+            recv_sem=ring_recv.at[side, hop - 1, q],
+            device_id={"blk": sides[side]},
+            device_id_type=MESH,
+        )
+
+    def local_copy(q):
+        return pltpu.make_async_copy(own_ref.at[q], all_ref.at[blk, q], local_sems.at[q])
+
+    def pair_sum(q, start):
+        mine = terms_ref[q, pl.ds(sec * 2 * group + start, group)].astype(jnp.float32)
+        return mine + got_core[q, pl.ds(start, group)].astype(jnp.float32)
+
+    def over_cores(q):
+        core_copy(q).wait_recv()
+        half[q] = pair_sum(q, other_ch * group).astype(jnp.bfloat16)
+        chip_copy(q).start()
+
+    def over_chips(q):
+        total = pair_sum(q, ch * group)
+        chip_copy(q).wait_recv()
+        own_ref[q] = (total + got_chip[q].astype(jnp.float32)).astype(jnp.bfloat16)
+        for side in range(2):
+            ring_copy(q, side, 1).start()
+        local_copy(q).start()
+
+    def forward(q, hop):
+        for side in range(2):
+            ring_copy(q, side, hop).wait_recv()
+            ring_copy(q, side, hop + 1).start()
+
+    events = []
+    for q in range(chunks):
+        events.append((2 * q, q, over_cores, (q,)))
+        events.append((2 * q + 2, q, over_chips, (q,)))
+        for hop in range(1, hops):
+            events.append((2 * q + 2 + hop, q, forward, (q, hop)))
+    for q in range(chunks):
+        core_copy(q).start()
+    for _, _, act, values in sorted(events, key=lambda event: event[:2]):
+        act(*values)
+    for q in range(chunks):
+        for side in range(2):
+            ring_copy(q, side, hops).wait_recv()
+    for q in range(chunks):
+        core_copy(q).wait_send()
+        chip_copy(q).wait_send()
+        local_copy(q).wait()
+        for side in range(2):
+            for hop in range(1, hops + 1):
+                ring_copy(q, side, hop).wait_send()
+
+
+def spread(terms):
+    n = lax.axis_size("blk")
+    chunks, chans, depth, lanes = terms.shape
+    group = chans // (lax.axis_size("sec") * lax.axis_size("ch"))
+    piece = (chunks, group, depth, lanes)
+    return pl.pallas_call(
+        functools.partial(spread_kernel, n),
+        in_specs=[pl.BlockSpec(memory_space=pltpu.VMEM)],
+        out_specs=[pl.BlockSpec(memory_space=pl.ANY), pl.BlockSpec(memory_space=pltpu.VMEM)],
+        out_shape=[
+            jax.ShapeDtypeStruct((n,) + piece, jnp.bfloat16),
+            jax.ShapeDtypeStruct(piece, jnp.bfloat16),
+        ],
+        scratch_shapes=[
+            pltpu.VMEM((chunks, 2 * group, depth, lanes), jnp.bfloat16),
+            pltpu.VMEM(piece, jnp.bfloat16),
+            pltpu.VMEM(piece, jnp.bfloat16),
+            pltpu.SemaphoreType.DMA((2, chunks)),
+            pltpu.SemaphoreType.DMA((2, chunks)),
+            pltpu.SemaphoreType.DMA((2, n // 2, chunks)),
+            pltpu.SemaphoreType.DMA((2, n // 2, chunks)),
+            pltpu.SemaphoreType.DMA((chunks,)),
+        ],
+        compiler_params=pltpu.CompilerParams(
+            collective_id=0, has_side_effects=True, vmem_limit_bytes=48 * 1024 * 1024
+        ),
+    )(terms)
+
+
 def pair_kernel(steps, local_ref, remote_ref, out_ref, lhs):
-    panel_len = local_ref.shape[2]
+    chunks, lanes = local_ref.shape[0], local_ref.shape[3]
+    panel_len = chunks * lanes
 
     @pl.when(pl.program_id(1) == 0)
     def _():
-        turned = local_ref[0].astype(jnp.float32).T
-        lhs[0:panel_len, :] = turned.astype(jnp.bfloat16)
-        other = jnp.concatenate([turned[:, steps:], -turned[:, :steps]], axis=1)
-        lhs[panel_len:, :] = other.astype(jnp.bfloat16)
-
-    sums = jnp.dot(lhs[...], remote_ref[0, 0], preferred_element_type=jnp.float32)
+        for q in range(chunks):
+            turned = local_ref[q, 0].astype(jnp.float32).T
+            lhs[q * lanes : (q + 1) * lanes, :] = turned.astype(jnp.bfloat16)
+            other = jnp.concatenate([turned[:, steps:], -turned[:, :steps]], axis=1)
+            low = panel_len + q * lanes
+            lhs[low : low + lanes, :] = other.astype(jnp.bfloat16)
+
+    remote = jnp.concatenate([remote_ref[0, q, 0] for q in range(chunks)], axis=1)
+    sums = jnp.dot(lhs[...], remote, preferred_element_type=jnp.float32)
     scaled = (sums * (1.0 / steps)).astype(jnp.bfloat16)
     out_ref[0, 0] = scaled[:panel_len]
     out_ref[0, 1] = scaled[panel_len:]
 
 
 def correlate(local, gathered):
-    chans, depth, panel_len = local.shape
-    panels = gathered.shape[0]
+    panels, chunks, chans, depth, lanes = gathered.shape
+    panel_len = chunks * lanes
     return pl.pallas_call(
         functools.partial(pair_kernel, depth // 2),
         grid=(chans, panels),
         in_specs=[
-            pl.BlockSpec((1, depth, panel_len), lambda c, j: (c, 0, 0)),
-            pl.BlockSpec((1, 1, depth, panel_len), lambda c, j: (j, c, 0, 0)),
+            pl.BlockSpec((chunks, 1, depth, lanes), lambda c, j: (0, c, 0, 0)),
+            pl.BlockSpec((1, chunks, 1, depth, lanes), lambda c, j: (j, 0, c, 0, 0)),
         ],
         out_specs=pl.BlockSpec((1, 2, panel_len, panel_len), lambda c, j: (c, 0, 0, j)),
         out_shape=jax.ShapeDtypeStruct((chans, 2, panel_len, panels * panel_len), jnp.bfloat16),
@@ -122,13 +267,8 @@
     table = dft_rows(first, span_len, FFT, chan_total, FFT // 2)
     weights = (window[:, None, :] * table[None]).astype(jnp.bfloat16)
     terms = filter_bank(voltages, weights.reshape(TAPS * 2 * chan_total, span_len))
-    spectra = lax.psum_scatter(
-        terms.reshape(chan_total, 2 * steps, panel_len),
-        ("sec", "ch"),
-        scatter_dimension=0,
-        tiled=True,
-    ).astype(jnp.bfloat16)
-    return correlate(spectra, lax.all_gather(spectra, "blk", axis=0))
+    gathered, own = spread(terms.reshape(panel_len // LANES, chan_total, 2 * steps, LANES))
+    return correlate(own, gathered)
 
 
 def solution(mesh):

time: 269 us -> 159 us (0.59)
  waiting for transfers between devices: 190 us -> 0 us
  Pallas kernels: 55.6 us -> 153 us
  between operations: 14.2 us -> 0.81 us
    all_gather x1 -> x0, waiting for transfers between devices: 119 us -> none  [body(): return correlate(spectra, lax.all_gather(spectra, 'blk', axis=0))]
    pallas_call x0 -> x1, Pallas kernels: none -> 99.8 us  [spread(): pl.pallas_call(functools.partial(spread_kernel, n), in_specs=[pl.BlockSpe...]
    reduce_scatter x1 -> x0, waiting for transfers between devices: 71.8 us -> none  [body(): lax.psum_scatter(terms.reshape(chan_total, 2 * steps, panel_len), ('sec',...]
  transfers between devices with their start and end apart: 2 -> 0, of which waited for: 2 -> 0; matrix products, arithmetic and copies ran while one was open for 0% -> 0% of each run, Pallas kernels for 0% -> 0%
where the time goes in v2:
time: 159 us
  Pallas kernels  153 us (96%)
  local copies, waits for them, and re-layouts  3.23 us (2%)
    pallas_call x1, Pallas kernels, spread(): pl.pallas_call(functools.partial(spread_kernel, n), in_specs=[pl.BlockSpe...  99.8 us
    pallas_call x1, Pallas kernels, filter_bank(): pl.pallas_call(functools.partial(bank_kernel, steps, chunk), grid=(panel_...  29.2 us
    pallas_call x1, Pallas kernels, correlate(): pl.pallas_call(functools.partial(pair_kernel, depth // 2), grid=(chans, p...  24.3 us
    unnamed x2, local copies, waits for them, and re-layouts  3.23 us

profile of v2, /device:TPU:0, one launch (start us, length us, event | category | flops | bytes accessed | tf_op | source)
XLA Modules:
  0.0 158.8 jit_solution(3614377475209181974)
XLA Ops:
  0.0 0.8 fusion.38
  1.6 0.3 fusion.5
  2.0 0.1 select_select_fusion
  2.1 0.1 multiply_add_fusion.1
  2.1 0.1 fusion.41
  2.3 29.2 %shard_map.17 = bf16[4,3840,128]{2,1,0:T(8,128)(2,1)S(1)} custom-call(bf16[123,512,512]{2,1,0:T(8,128)(2,1)} %volts_ref.1, bf16[128,512]{1,0:T(8,128)(2,1)S(1)} %bitcast.3), custom_call_target="tpu_custom_call" | custom-call | tf_op jit(solution)/shard_map/pallas_call | solution.py:72
  31.5 99.8 %shard_map.18 = (bf16[8,4,4,240,128]{4,3,2,1,0:T(8,128)(2,1)}, bf16[4,4,240,128]{3,2,1,0:T(8,128)(2,1)S(1)}) custom-call(bf16[4,16,240,128]{3,2,1,0:T(8,128)(2,1)S(1)} %bitcast.2), custom_call_target="tpu_custom_call" | custom-call | tf_op jit(solution)/shard_map/pallas_call | solution.py:198
  131.3 0.0 copy-start
  131.3 3.2 %copy-done = bf16[8,4,4,240,128]{4,3,2,1,0:T(8,128)(2,1)S(1)} copy-done((bf16[8,4,4,240,128]{4,3,2,1,0:T(8,128)(2,1)S(1)}, bf16[8,4,4,240,128]{4,3,2,1,0:T(8,128)(2,1)}, u32[]{:S(2)}) %copy-start) | copy-done | bytes 7864344
  134.6 24.3 %shard_map.19 = bf16[4,2,512,4096]{3,2,1,0:T(8,128)(2,1)} custom-call(bf16[4,4,240,128]{3,2,1,0:T(8,128)(2,1)S(1)} %get-tuple-element.7.local_ref, bf16[8,4,4,240,128]{4,3,2,1,0:T(8,128)(2,1)S(1)} %copy-done), custom_call_target="tpu_custom_call" | custom-call | tf_op jit(solution)/shard_map/pallas_call | solution.py:245
  (6 shorter events, 0.1 us)
Async XLA Ops:
  131.3 3.2 %copy-start = (bf16[8,4,4,240,128]{4,3,2,1,0:T(8,128)(2,1)S(1)}, bf16[8,4,4,240,128]{4,3,2,1,0:T(8,128)(2,1)}, u32[]{:S(2)}) copy-start(bf16[8,4,4,240,128]{4,3,2,1,0:T(8,128)(2,1)} %get-tuple-element.8.remote_ref) | copy-start | bytes 23592964

commit v3 on v2

--- a/solution.py
+++ b/solution.py
@@ -36,63 +36,16 @@
     return wave.astype(jnp.bfloat16).astype(jnp.float32)
 
 
-def bank_kernel(steps, chunk, volts_ref, weights_ref, out_ref, products, spectra):
-    part = pl.program_id(1)
-    rows = weights_ref.shape[0] // TAPS
-    weights = weights_ref[...]
-
-    for frame in range(chunk):
-        products[part * chunk + frame] = lax.dot_general(
-            weights,
-            volts_ref[frame],
-            (((1,), (1,)), ((), ())),
-            preferred_element_type=jnp.float32,
-        )
-
-    def add_taps(step, carry):
-        total = products[step, 0:rows]
-        for tap in range(1, TAPS):
-            total = total + products[step + tap, tap * rows : (tap + 1) * rows]
-        spectra[pl.ds(step, rows, stride=steps), :] = total
-        return carry
-
-    low = jnp.maximum(part * chunk - (TAPS - 1), 0)
-    lax.fori_loop(low, (part + 1) * chunk - (TAPS - 1), add_taps, 0)
-
-    @pl.when(part == pl.num_programs(1) - 1)
-    def _():
-        out_ref[0] = spectra[...].astype(jnp.bfloat16)
-
-
-def filter_bank(voltages, weights):
-    frames, panel_len, span_len = voltages.shape
-    steps = frames - TAPS + 1
-    rows = weights.shape[0] // TAPS
-    chunk = next(size for size in (41, 3, 1) if frames % size == 0)
-    return pl.pallas_call(
-        functools.partial(bank_kernel, steps, chunk),
-        grid=(panel_len // LANES, frames // chunk),
-        in_specs=[
-            pl.BlockSpec((chunk, LANES, span_len), lambda s, f: (f, s, 0)),
-            pl.BlockSpec(weights.shape, lambda s, f: (0, 0)),
-        ],
-        out_specs=pl.BlockSpec((1, rows * steps, LANES), lambda s, f: (s, 0, 0)),
-        out_shape=jax.ShapeDtypeStruct((panel_len // LANES, rows * steps, LANES), jnp.bfloat16),
-        scratch_shapes=[
-            pltpu.VMEM((frames, weights.shape[0], LANES), jnp.float32),
-            pltpu.VMEM((rows * steps, LANES), jnp.float32),
-        ],
-        compiler_params=pltpu.CompilerParams(vmem_limit_bytes=48 * 1024 * 1024),
-    )(voltages, weights)
-
-
-def spread_kernel(n, terms_ref, all_ref, own_ref, got_core, half, got_chip, core_sems, chip_sems,
-                  ring_send, ring_recv, local_sems):
+def spread_kernel(n, volts_ref, weights_ref, all_ref, own_ref, volts, products, spectra, terms_ref, got_core,
+                  half, got_chip, volts_sems, core_sems, chip_sems, ring_send, ring_recv, local_sems):
     sec, ch, blk = lax.axis_index("sec"), lax.axis_index("ch"), lax.axis_index("blk")
     other_sec, other_ch = 1 - sec, 1 - ch
     chunks = terms_ref.shape[0]
     group = own_ref.shape[1]
     hops = n // 2
+    frames, part_len = volts_ref.shape[0], volts.shape[1]
+    parts, steps = frames // part_len, frames - TAPS + 1
+    rows = weights_ref.shape[0] // TAPS
 
     def block_at(place):
         place = lax.rem(place + 2 * n, n)
@@ -105,7 +58,56 @@
     partners = ({"sec": other_sec}, {"ch": other_ch}, {"blk": sides[0]}, {"blk": sides[1]})
     for partner in partners:
         pl.semaphore_signal(barrier, inc=1, device_id=partner, device_id_type=MESH)
-    pl.semaphore_wait(barrier, len(partners))
+
+    def volts_copy(index):
+        slot = lax.rem(index, 2)
+        return pltpu.make_async_copy(
+            volts_ref.at[
+                pl.ds(lax.rem(index, parts) * part_len, part_len), pl.ds(index // parts * LANES, LANES)
+            ],
+            volts.at[slot],
+            volts_sems.at[slot],
+        )
+
+    def produce(q, extras):
+        def one_part(part, carry):
+            index = q * parts + part
+            slot = lax.rem(index, 2)
+            volts_copy(index).wait()
+
+            @pl.when(index + 1 < chunks * parts)
+            def _():
+                volts_copy(index + 1).start()
+
+            weights = weights_ref[...]
+            for frame in range(part_len):
+                products[part * part_len + frame] = lax.dot_general(
+                    weights,
+                    volts[slot, frame],
+                    (((1,), (1,)), ((), ())),
+                    preferred_element_type=jnp.float32,
+                )
+
+            def add_taps(step, carry):
+                total = products[step, 0:rows]
+                for tap in range(1, TAPS):
+                    total = total + products[step + tap, tap * rows : (tap + 1) * rows]
+                spectra[pl.ds(step, rows, stride=steps), :] = total
+                return carry
+
+            low = jnp.maximum(part * part_len - (TAPS - 1), 0)
+            lax.fori_loop(low, (part + 1) * part_len - (TAPS - 1), add_taps, 0)
+
+            for place_in_bank, acts in extras.items():
+                @pl.when(part == place_in_bank)
+                def _():
+                    for act, values in acts:
+                        act(*values)
+
+            return carry
+
+        lax.fori_loop(0, parts, one_part, 0)
+        terms_ref[q] = spectra[...].reshape(terms_ref.shape[1:]).astype(jnp.bfloat16)
 
     def core_copy(q):
         return pltpu.make_async_remote_copy(
@@ -170,13 +172,25 @@
 
     events = []
     for q in range(chunks):
-        events.append((2 * q, q, over_cores, (q,)))
+        events.append((2 * q - 1, q, over_cores, (q,)))
         events.append((2 * q + 2, q, over_chips, (q,)))
         for hop in range(1, hops):
             events.append((2 * q + 2 + hop, q, forward, (q, hop)))
+    events = [event[2:] for event in sorted(events, key=lambda event: event[:2])]
+
+    volts_copy(0).start()
     for q in range(chunks):
+        early = [(over_cores, (q - 1,)), (over_chips, (q - 2,)), (forward, (q - 3, 1))]
+        late = [(forward, (q - 3, 2))]
+        early = [event for event in early if event in events]
+        late = [event for event in late if event in events]
+        events = [event for event in events if event not in early + late]
+        extras = {0: early + late} if parts == 1 else {0: early, parts - 1: late}
+        produce(q, {part: acts for part, acts in extras.items() if acts})
+        if q == 0:
+            pl.semaphore_wait(barrier, len(partners))
         core_copy(q).start()
-    for _, _, act, values in sorted(events, key=lambda event: event[:2]):
+    for act, values in events:
         act(*values)
     for q in range(chunks):
         for side in range(2):
@@ -190,23 +204,32 @@
                 ring_copy(q, side, hop).wait_send()
 
 
-def spread(terms):
+def spread(voltages, weights):
     n = lax.axis_size("blk")
-    chunks, chans, depth, lanes = terms.shape
-    group = chans // (lax.axis_size("sec") * lax.axis_size("ch"))
+    frames, panel_len, span_len = voltages.shape
+    steps = frames - TAPS + 1
+    rows = weights.shape[0] // TAPS
+    chunks, lanes, depth = panel_len // LANES, LANES, 2 * steps
+    part_len = next(size for size in (41, 3, 1) if frames % size == 0)
+    group = rows // 2 // (lax.axis_size("sec") * lax.axis_size("ch"))
     piece = (chunks, group, depth, lanes)
     return pl.pallas_call(
         functools.partial(spread_kernel, n),
-        in_specs=[pl.BlockSpec(memory_space=pltpu.VMEM)],
+        in_specs=[pl.BlockSpec(memory_space=pl.ANY), pl.BlockSpec(memory_space=pltpu.VMEM)],
         out_specs=[pl.BlockSpec(memory_space=pl.ANY), pl.BlockSpec(memory_space=pltpu.VMEM)],
         out_shape=[
             jax.ShapeDtypeStruct((n,) + piece, jnp.bfloat16),
             jax.ShapeDtypeStruct(piece, jnp.bfloat16),
         ],
         scratch_shapes=[
+            pltpu.VMEM((2, part_len, lanes, span_len), jnp.bfloat16),
+            pltpu.VMEM((frames, weights.shape[0], lanes), jnp.float32),
+            pltpu.VMEM((rows * steps, lanes), jnp.float32),
+            pltpu.VMEM((chunks, rows // 2, depth, lanes), jnp.bfloat16),
             pltpu.VMEM((chunks, 2 * group, depth, lanes), jnp.bfloat16),
             pltpu.VMEM(piece, jnp.bfloat16),
             pltpu.VMEM(piece, jnp.bfloat16),
+            pltpu.SemaphoreType.DMA((2,)),
             pltpu.SemaphoreType.DMA((2, chunks)),
             pltpu.SemaphoreType.DMA((2, chunks)),
             pltpu.SemaphoreType.DMA((2, n // 2, chunks)),
@@ -214,9 +237,9 @@
             pltpu.SemaphoreType.DMA((chunks,)),
         ],
         compiler_params=pltpu.CompilerParams(
-            collective_id=0, has_side_effects=True, vmem_limit_bytes=48 * 1024 * 1024
+            collective_id=0, has_side_effects=True, vmem_limit_bytes=56 * 1024 * 1024
         ),
-    )(terms)
+    )(voltages, weights)
 
 
 def pair_kernel(steps, local_ref, remote_ref, out_ref, lhs):
@@ -232,27 +255,30 @@
             low = panel_len + q * lanes
             lhs[low : low + lanes, :] = other.astype(jnp.bfloat16)
 
-    remote = jnp.concatenate([remote_ref[0, q, 0] for q in range(chunks)], axis=1)
-    sums = jnp.dot(lhs[...], remote, preferred_element_type=jnp.float32)
-    scaled = (sums * (1.0 / steps)).astype(jnp.bfloat16)
-    out_ref[0, 0] = scaled[:panel_len]
-    out_ref[0, 1] = scaled[panel_len:]
+    for place in range(remote_ref.shape[0]):
+        remote = jnp.concatenate([remote_ref[place, q, 0] for q in range(chunks)], axis=1)
+        sums = jnp.dot(lhs[...], remote, preferred_element_type=jnp.float32)
+        scaled = (sums * (1.0 / steps)).astype(jnp.bfloat16)
+        span = slice(place * panel_len, (place + 1) * panel_len)
+        out_ref[0, 0, :, span] = scaled[:panel_len]
+        out_ref[0, 1, :, span] = scaled[panel_len:]
 
 
 def correlate(local, gathered):
     panels, chunks, chans, depth, lanes = gathered.shape
     panel_len = chunks * lanes
+    batch = 2 if panels % 2 == 0 else 1
     return pl.pallas_call(
         functools.partial(pair_kernel, depth // 2),
-        grid=(chans, panels),
+        grid=(chans, panels // batch),
         in_specs=[
             pl.BlockSpec((chunks, 1, depth, lanes), lambda c, j: (0, c, 0, 0)),
-            pl.BlockSpec((1, chunks, 1, depth, lanes), lambda c, j: (j, 0, c, 0, 0)),
+            pl.BlockSpec((batch, chunks, 1, depth, lanes), lambda c, j: (j, 0, c, 0, 0)),
         ],
-        out_specs=pl.BlockSpec((1, 2, panel_len, panel_len), lambda c, j: (c, 0, 0, j)),
+        out_specs=pl.BlockSpec((1, 2, panel_len, batch * panel_len), lambda c, j: (c, 0, 0, j)),
         out_shape=jax.ShapeDtypeStruct((chans, 2, panel_len, panels * panel_len), jnp.bfloat16),
         scratch_shapes=[pltpu.VMEM((2 * panel_len, depth), jnp.bfloat16)],
-        compiler_params=pltpu.CompilerParams(vmem_limit_bytes=32 * 1024 * 1024),
+        compiler_params=pltpu.CompilerParams(vmem_limit_bytes=56 * 1024 * 1024),
     )(local, gathered)
 
 
@@ -266,8 +292,7 @@
     window = lax.dynamic_slice_in_dim(make_window(TAPS, FFT), first, span_len, 1)
     table = dft_rows(first, span_len, FFT, chan_total, FFT // 2)
     weights = (window[:, None, :] * table[None]).astype(jnp.bfloat16)
-    terms = filter_bank(voltages, weights.reshape(TAPS * 2 * chan_total, span_len))
-    gathered, own = spread(terms.reshape(panel_len // LANES, chan_total, 2 * steps, LANES))
+    gathered, own = spread(voltages, weights.reshape(TAPS * 2 * chan_total, span_len))
     return correlate(own, gathered)
 
 

time: 159 us -> 138 us (0.87)
  Pallas kernels: 153 us -> 135 us
  local copies, waits for them, and re-layouts: 3.23 us -> 0 us
    pallas_call x1 -> x0, Pallas kernels: 29.2 us -> none  [filter_bank(): pl.pallas_call(functools.partial(bank_kernel, steps, chunk), grid=(panel_...]
    pallas_call x1, Pallas kernels: 99.8 us -> 113 us  [spread(): pl.pallas_call(functools.partial(spread_kernel, n), in_specs=[pl.BlockSpe...]
    unnamed x2 -> x0, local copies, waits for them, and re-layouts: 3.23 us -> none
    pallas_call x1, Pallas kernels: 24.3 us -> 21.8 us  [correlate(): pl.pallas_call(functools.partial(pair_kernel, depth // 2), grid=(chans, p...]
where the time goes in v3:
time: 138 us; the launch traced here: 137 us
  Pallas kernels  135 us (98%)
  other arithmetic  2.13 us (2%)
    pallas_call x1, Pallas kernels, spread(): pl.pallas_call(functools.partial(spread_kernel, n), in_specs=[pl.BlockSpe...  113 us
    pallas_call x1, Pallas kernels, correlate(): pl.pallas_call(functools.partial(pair_kernel, depth // 2), grid=(chans, p...  21.8 us

profile of v3, /device:TPU:0, one launch (start us, length us, event | category | flops | bytes accessed | tf_op | source)
XLA Modules:
  0.0 137.5 jit_solution(4244165081995184686)
XLA Ops:
  0.0 0.8 fusion.38
  1.6 0.3 fusion.5
  2.0 0.1 select_select_fusion
  2.1 0.1 multiply_add_fusion.1
  2.1 0.1 fusion.41
  2.2 0.7 multiply_convert_fusion
  2.9 112.8 %shard_map.17 = (bf16[8,4,4,240,128]{4,3,2,1,0:T(8,128)(2,1)}, bf16[4,4,240,128]{3,2,1,0:T(8,128)(2,1)}) custom-call(bf16[123,512,512]{2,1,0:T(8,128)(2,1)} %volts_ref.1, bf16[128,512]{1,0:T(8,128)(2,1)} %bitcast.1), custom_call_target="tpu_custom_call" | custom-call | tf_op jit(solution)/shard_map/pallas_call | solution.py:216
  115.7 21.8 %shard_map.18 = bf16[4,2,512,4096]{3,2,1,0:T(8,128)(2,1)} custom-call(bf16[4,4,240,128]{3,2,1,0:T(8,128)(2,1)} %get-tuple-element.7.local_ref, bf16[8,4,4,240,128]{4,3,2,1,0:T(8,128)(2,1)} %get-tuple-element.8.remote_ref), custom_call_target="tpu_custom_call" | custom-call | tf_op jit(solution)/shard_map/pallas_call | solution.py:271
  (5 shorter events, 0.1 us)

commit v4 on v3

--- a/solution.py
+++ b/solution.py
@@ -267,7 +267,7 @@
 def correlate(local, gathered):
     panels, chunks, chans, depth, lanes = gathered.shape
     panel_len = chunks * lanes
-    batch = 2 if panels % 2 == 0 else 1
+    batch = 8 if panels % 8 == 0 else 1
     return pl.pallas_call(
         functools.partial(pair_kernel, depth // 2),
         grid=(chans, panels // batch),

time: 138 us -> 133 us (0.964)
  Pallas kernels: 135 us -> 130 us
    pallas_call x1, Pallas kernels: 21.8 us -> 17 us  [correlate(): pl.pallas_call(functools.partial(pair_kernel, depth // 2), grid=(chans, p...]
where the time goes in v4:
time: 133 us
  Pallas kernels  130 us (98%)
  other arithmetic  2.13 us (2%)
    pallas_call x1, Pallas kernels, spread(): pl.pallas_call(functools.partial(spread_kernel, n), in_specs=[pl.BlockSpe...  113 us
    pallas_call x1, Pallas kernels, correlate(): pl.pallas_call(functools.partial(pair_kernel, depth // 2), grid=(chans, p...  17 us

profile of v4, /device:TPU:0, one launch (start us, length us, event | category | flops | bytes accessed | tf_op | source)
XLA Modules:
  0.0 132.7 jit_solution(16324710261750891848)
XLA Ops:
  0.0 0.8 fusion.38
  1.6 0.3 fusion.5
  2.0 0.1 select_select_fusion
  2.1 0.1 multiply_add_fusion.1
  2.1 0.1 fusion.41
  2.2 0.7 multiply_convert_fusion
  2.9 112.8 %shard_map.17 = (bf16[8,4,4,240,128]{4,3,2,1,0:T(8,128)(2,1)}, bf16[4,4,240,128]{3,2,1,0:T(8,128)(2,1)}) custom-call(bf16[123,512,512]{2,1,0:T(8,128)(2,1)} %volts_ref.1, bf16[128,512]{1,0:T(8,128)(2,1)} %bitcast.1), custom_call_target="tpu_custom_call" | custom-call | tf_op jit(solution)/shard_map/pallas_call | solution.py:216
  115.7 17.0 %shard_map.18 = bf16[4,2,512,4096]{3,2,1,0:T(8,128)(2,1)} custom-call(bf16[4,4,240,128]{3,2,1,0:T(8,128)(2,1)} %get-tuple-element.7.local_ref, bf16[8,4,4,240,128]{4,3,2,1,0:T(8,128)(2,1)} %get-tuple-element.8.remote_ref), custom_call_target="tpu_custom_call" | custom-call | tf_op jit(solution)/shard_map/pallas_call | solution.py:271
  (5 shorter events, 0.1 us)
